TPU v7x, 256 devices: a whole 4x4x8 slice. The times are simulated.
256 devices in a mesh: chan: 2 (over x_lo), elem: 8 (over y, x_hi), beam: 16 (over z, core).
Axes of the slice: x: 4 (x_hi: 2, x_lo: 2; x = x_hi * 2 + x_lo), y: 4, z: 8, core: 2. Of those that a mesh axis runs over, the one named last changes fastest.
Arguments:
- voltages: bfloat16 [2, 128, 256, 2048], P(None, 'chan', 'beam', 'elem'), may hold values from -6 to 6
- weights: bfloat16 [2, 128, 2048, 2048], P(None, 'chan', 'elem', 'beam'), may hold values from -0.09375 to 0.09375
Outputs:
- power: float32 [128, 256, 2048], P(None, ('chan', 'elem'), 'beam')
All inputs are finite; a program needn't handle non-finite values.
Results may differ from a plain program's by a relative error of at most 0.012.
Values may be sent and summed in bfloat16 or wider, within the bound.
A program may use at most 128 MiB of HBM per device.

v0:
```python
import jax
import jax.numpy as jnp
from jax import lax
from jax.sharding import PartitionSpec as P


def dft_tables(channels):
    index = jnp.arange(channels, dtype=jnp.int32)
    phase = index[:, None] * index[None, :] % channels
    angle = phase.astype(jnp.float32) * (2.0 * jnp.pi / channels)
    factor = 1.0 / jnp.sqrt(jnp.float32(channels))
    return (jnp.cos(angle) * factor, jnp.sin(angle) * factor)


def shards(voltages, weights):
    local_beams = weights.shape[3]
    volt_piece = lax.all_gather(voltages, "beam", axis=2, tiled=True)
    real_part = jnp.einsum(
        "cte,ceb->ctb", volt_piece[0], weights[0], preferred_element_type=jnp.float32
    ) - jnp.einsum("cte,ceb->ctb", volt_piece[1], weights[1], preferred_element_type=jnp.float32)
    imag_part = jnp.einsum(
        "cte,ceb->ctb", volt_piece[0], weights[1], preferred_element_type=jnp.float32
    ) + jnp.einsum("cte,ceb->ctb", volt_piece[1], weights[0], preferred_element_type=jnp.float32)
    partial_value = jnp.stack([real_part, imag_part])
    summed = lax.psum_scatter(
        partial_value.astype(jnp.bfloat16), "elem", scatter_dimension=1, tiled=True
    )
    owned = lax.all_to_all(summed, ("chan", "elem"), split_axis=2, concat_axis=1, tiled=True)
    channels = owned.shape[1]
    own_time = owned.shape[2]
    cosine, sine = dft_tables(channels)
    real_in = owned[0].astype(jnp.float32).reshape(channels, own_time * local_beams)
    imag_in = owned[1].astype(jnp.float32).reshape(channels, own_time * local_beams)
    highest = lax.Precision.HIGHEST
    real_out = jnp.dot(
        cosine, real_in, precision=highest, preferred_element_type=jnp.float32
    ) - jnp.dot(sine, imag_in, precision=highest, preferred_element_type=jnp.float32)
    imag_out = jnp.dot(
        sine, real_in, precision=highest, preferred_element_type=jnp.float32
    ) + jnp.dot(cosine, imag_in, precision=highest, preferred_element_type=jnp.float32)
    power = real_out * real_out + imag_out * imag_out
    return power.reshape(channels, own_time, local_beams)


def solution(mesh):
    placed = (P(None, "chan", "beam", "elem"), P(None, "chan", "elem", "beam"))
    return jax.shard_map(
        shards,
        mesh=mesh,
        in_specs=placed,
        out_specs=P(None, ("chan", "elem"), "beam"),
        check_vma=False,
    )
```

profile of v0, /device:TPU:8, one launch (start us, length us, event | category | flops | bytes accessed | tf_op | source)
XLA Modules:
  0.0 327.8 jit_solution(3343616162390138863)
XLA Ops:
  6.5 0.0 all-gather.2.cloned.1.call-start
  6.5 0.7 all-gather.2.cloned.1.call-update
  7.3 0.0 reduce-scatter.5.cloned.1.call-start
  7.3 100.1 %all-gather.2.cloned.1.call-done = bf16[2,64,256,256]{3,2,1,0:T(8,128)(2,1)} async-done(((bf16[2,64,16,256]{3,2,1,0:T(8,128)(2,1)}), bf16[2,64,256,256]{3,2,1,0:T(8,128)(2,1)}) %all-gather.2.cloned.1.call-update) | async-done | bytes 16777232 | tf_op jit(solution)/shard_map/all_gather | solution.py:17
  107.4 10.1 %fusion = f32[64,256,128]{2,1,0:T(8,128)} fusion(bf16[2,64,256,256]{3,2,1,0:T(8,128)(2,1)} %all-gather.2.cloned.1.call-done, bf16[2,64,256,128]{3,2,1,0:T(8,128)(2,1)} %param.3), kind=kOutput, calls=%fused_computation.6 | convolution fusion | flops 1073741824 | bytes 20971520 | tf_op jit(solution)/shard_map/cte,ceb->ctb/dot_general | solution.py:21
  117.6 10.1 %fusion.1 = f32[64,256,128]{2,1,0:T(8,128)} fusion(bf16[2,64,256,256]{3,2,1,0:T(8,128)(2,1)} %all-gather.2.cloned.1.call-done, bf16[2,64,256,128]{3,2,1,0:T(8,128)(2,1)} %param.3), kind=kOutput, calls=%fused_computation.7 | convolution fusion | flops 1073741824 | bytes 20971520 | tf_op jit(solution)/shard_map/cte,ceb->ctb/dot_general | solution.py:18
  127.7 11.4 %fusion.5 = bf16[1,64,256,128]{3,2,1,0:T(8,128)(2,1)} fusion(f32[64,256,128]{2,1,0:T(8,128)} %fusion, bf16[2,64,256,128]{3,2,1,0:T(8,128)(2,1)} %param.3, bf16[2,64,256,256]{3,2,1,0:T(8,128)(2,1)} %all-gather.2.cloned.1.call-done), kind=kOutput, calls=%fused_computation.11 | convolution fusion | flops 1077936128 | bytes 25165824 | tf_op jit(solution)/shard_map/cte,ceb->ctb/dot_general | solution.py:23
  139.1 11.3 %fusion.4 = bf16[1,64,256,128]{3,2,1,0:T(8,128)(2,1)} fusion(f32[64,256,128]{2,1,0:T(8,128)} %fusion.1, bf16[2,64,256,128]{3,2,1,0:T(8,128)(2,1)} %param.3, bf16[2,64,256,256]{3,2,1,0:T(8,128)(2,1)} %all-gather.2.cloned.1.call-done), kind=kOutput, calls=%fused_computation.10 | convolution fusion | flops 1077936128 | bytes 25165824 | tf_op jit(solution)/shard_map/cte,ceb->ctb/dot_general | solution.py:20
  150.4 7.4 %pad_maximum_fusion = bf16[2,64,256,128]{3,2,1,0:T(8,128)(2,1)} fusion(bf16[1,64,256,128]{3,2,1,0:T(8,128)(2,1)} %fusion.5, bf16[1,64,256,128]{3,2,1,0:T(8,128)(2,1)} %fusion.4), kind=kLoop, calls=%fused_computation.3 | loop fusion | flops 4194304 | bytes 16777216 | tf_op jit(solution)/shard_map/stack | solution.py:24
  157.9 7.7 %copy.6 = bf16[2,64,256,128]{3,2,0,1:T(8,128)(2,1)} copy(bf16[2,64,256,128]{3,2,1,0:T(8,128)(2,1)} %pad_maximum_fusion) | data formatting | bytes 16777216
  165.6 12.2 %copy.33 = bf16[8,8,512,128]{3,1,2,0:T(8,128)(2,1)} copy(bf16[8,8,512,128]{3,2,1,0:T(8,128)(2,1)} %bitcast.69) | data formatting | bytes 16777216
  177.8 0.0 reduce-scatter.5.cloned.1.call-update
  177.8 117.0 %reduce-scatter.5.cloned.1.call-done = bf16[8,65536]{1,0:T(8,128)(2,1)} async-done(((bf16[64,65536]{1,0:T(8,128)(2,1)}), bf16[8,65536]{1,0:T(8,128)(2,1)}) %reduce-scatter.5.cloned.1.call-update) | async-done | bytes 1048592
  294.8 1.4 copy.4
  296.2 19.6 %all_to_all.15 = bf16[2,8,256,128]{3,1,0,2:T(8,128)(2,1)S(1)} all-to-all(bf16[2,8,256,128]{3,1,0,2:T(8,128)(2,1)S(1)} %copy.4), channel_id=1, replica_groups=mesh['chan'=2,'elem'=8,'beam'=16] {'chan','elem'}, dimensions={2} | all-to-all | bytes 2097152 | tf_op jit(solution)/shard_map/all_to_all | solution.py:28
  315.8 0.3 copy.34
  316.1 0.3 slice_bitcast_fusion.10
  316.4 0.8 fusion.24
  317.2 0.8 fusion.26
  318.1 0.8 fusion.16
  318.9 0.9 fusion.21
  319.8 1.2 copy.13
Async XLA Ops:
  6.5 100.9 %all-gather.2.cloned.1.call-start = ((), (), s32[]{:S(2)}) async-start(), calls=%async_computation.2 | async-start | bytes 17825792 | tf_op jit(solution)/shard_map/all_gather | solution.py:17
  7.3 287.5 %reduce-scatter.5.cloned.1.call-start = ((), (), s32[]{:S(2)}) async-start(), calls=%async_computation.3 | async-start | bytes 9437184
Sparse Core Ops, SparseCore 0:
  9.2 98.2 all-gather.1
  177.9 116.8 reduce-scatter.4
where the time goes:
time: 329 us; the launch traced here: 328 us
  waiting for transfers between devices  218 us (66%)
  matrix products  46.4 us (14%)
  local copies, waits for them, and re-layouts  23 us (7%)
  blocking collectives  19.6 us (6%)
  between operations  13.4 us (4%)
  other arithmetic  7.45 us (2%)
    unnamed x3, waiting for transfers between devices  118 us
    all_gather x1, waiting for transfers between devices, shards(): volt_piece = lax.all_gather(voltages, 'beam', axis=2, tiled=True)  100 us
    unnamed x4, local copies, waits for them, and re-layouts  21.3 us
    all_to_all x1, blocking collectives, shards(): lax.all_to_all(summed, ('chan', 'elem'), split_axis=2, concat_axis=1, til...  19.6 us
    dot_general x1, matrix products, shards(): jnp.einsum('cte,ceb->ctb', volt_piece[1], weights[0], preferred_element_t...  11.4 us
    dot_general x1, matrix products, shards(): jnp.einsum('cte,ceb->ctb', volt_piece[1], weights[1], preferred_element_t...  11.3 us
    dot_general x1, matrix products, shards(): jnp.einsum('cte,ceb->ctb', volt_piece[0], weights[0], preferred_element_t...  10.1 us
    dot_general x1, matrix products, shards(): jnp.einsum('cte,ceb->ctb', volt_piece[0], weights[1], preferred_element_t...  10.1 us
  transfers between devices with their start and end apart: 2, of which 2 were waited for; matrix products, arithmetic and copies ran while one was open for 0% of the time, Pallas kernels for 0%

commit v1 on v0

v1 whole, which is shorter than its diff:
```python
import functools

import jax
import jax.numpy as jnp
import numpy as np
from jax import lax
from jax.experimental import pallas as pl
from jax.experimental.pallas import tpu as pltpu
from jax.sharding import PartitionSpec as P

MESH = pl.DeviceIdType.MESH

X, Y, Z = 4, 4, 8
CHUNKS = 16


def synthesis_table(channels):
    index = np.arange(channels)
    angle = (index[:, None] * index[None, :] % channels) * (2.0 * np.pi / channels)
    cosine, sine = np.cos(angle) / np.sqrt(channels), np.sin(angle) / np.sqrt(channels)
    table = np.block([[cosine, -sine], [sine, cosine]]).astype(np.float32)
    high = table.astype(jnp.bfloat16)
    low = (table - high.astype(np.float32)).astype(jnp.bfloat16)
    return np.concatenate([high, low], axis=0)


def kernel(
    volt_hbm, weight_hbm, table_ref, power_ref,
    volt, weight, part, early, late, cross, spread,
    volt_in, weight_in, z_recv, mate_recv, early_recv, late_recv, cross_recv,
    z_send, mate_send, y_send, x_send,
):
    chan, elem, beam = lax.axis_index("chan"), lax.axis_index("elem"), lax.axis_index("beam")
    z, core = beam // 2, beam % 2
    y, x_hi = elem // 2, elem % 2
    x = x_hi * 2 + chan
    per = volt.shape[1] // CHUNKS
    times = volt.shape[3]
    channels = 2 * volt.shape[1]

    def at_z(step):
        return (chan, elem, lax.rem(z + step + Z, Z) * 2 + core)

    def at_y(step):
        return (chan, lax.rem(y + step + Y, Y) * 2 + x_hi, beam)

    def at_x(step):
        to = lax.rem(x + step, X)
        return (to % 2, y * 2 + to // 2, beam)

    mate = (chan, elem, z * 2 + (1 - core))
    others = [mate, at_z(1), at_z(-1), at_y(1), at_y(-1), at_x(1), at_x(2), at_x(3)]

    def fetch_volt(k):
        at = pl.ds(k * per, per)
        return pltpu.make_async_copy(volt_hbm.at[:, at], volt.at[:, at, beam], volt_in.at[k])

    def fetch_weight(k):
        at = pl.ds(k * per, per)
        return pltpu.make_async_copy(weight_hbm.at[:, at], weight.at[:, at], weight_in.at[k])

    def send(src, dst, send_sem, recv_sem, to):
        pltpu.make_async_remote_copy(
            src_ref=src, dst_ref=dst, send_sem=send_sem, recv_sem=recv_sem, device_id=to, device_id_type=MESH
        ).start()

    def await_bytes(like, sem):
        pltpu.make_async_copy(like, like, sem).wait()

    def piece(k, owner, half=None):
        at = pl.ds(k * per, per)
        if half is None:
            return volt.at[:, at, owner]
        return volt.at[half, at, owner]

    def owner_of(side, distance):
        step = -distance if side == 0 else distance
        return lax.rem(z + step + Z, Z) * 2 + core

    def z_hop(k, side, distance):
        owner = owner_of(side, distance)
        half = side if distance == 4 else None
        if distance:
            here = piece(k, owner, half)
            await_bytes(here, z_recv.at[side, distance - 1, k])
        if distance < 4:
            there = piece(k, owner, side if distance == 3 else None)
            send(there, there, z_send.at[side], z_recv.at[side, distance, k], at_z(1 if side == 0 else -1))
        if distance or side == 0:
            here = piece(k, owner, half)
            send(here, here, mate_send, mate_recv.at[k], mate)

    def to_y(step):
        return lax.rem(y + step + Y, Y)

    def multiply(k):
        fetch_weight(k).wait()
        await_bytes(volt.at[:, pl.ds(k * per, per), pl.ds(0, 8)], mate_recv.at[k])

        @pl.loop(0, per)
        def _(c):
            at = k * per + c
            rows = volt.shape[2] * times
            width = volt.shape[4]
            volt_real = volt[0, at].reshape(rows, width)
            volt_imag = volt[1, at].reshape(rows, width)
            both = jnp.concatenate([weight[0, at], weight[1, at]], axis=1)
            beams = weight.shape[3]
            with_real = jnp.dot(volt_real, both, preferred_element_type=jnp.float32)
            with_imag = jnp.dot(volt_imag, both, preferred_element_type=jnp.float32)
            real = with_real[:, :beams] - with_imag[:, beams:]
            imag = with_real[:, beams:] + with_imag[:, :beams]
            shape = part.shape[3:]
            part[k, 0, c] = real.astype(jnp.bfloat16).reshape(shape)
            part[k, 1, c] = imag.astype(jnp.bfloat16).reshape(shape)

    def send_early(k):
        far = to_y(2)
        for side in (0, 1):
            send(
                part.at[k, side, :, :, far], early.at[k, side], y_send.at[side], early_recv.at[side, k],
                at_y(1 if side == 0 else -1),
            )

    def send_late(k):
        for side in (0, 1):
            near = to_y(1 if side == 0 else -1)
            await_bytes(early.at[k, side], early_recv.at[side, k])
            for c in range(per):
                total = part[k, side, c, :, near].astype(jnp.float32) + early[k, side, c].astype(jnp.float32)
                part[k, side, c, :, near] = total.astype(jnp.bfloat16)
            send(
                part.at[k, :, :, :, near], late.at[k, side], y_send.at[side], late_recv.at[side, k],
                at_y(1 if side == 0 else -1),
            )

    def send_cross(k):
        for side in (0, 1):
            await_bytes(late.at[k, side], late_recv.at[side, k])
        for ri in (0, 1):
            for c in range(per):
                total = (
                    part[k, ri, c, :, y].astype(jnp.float32)
                    + late[k, 0, ri, c].astype(jnp.float32)
                    + late[k, 1, ri, c].astype(jnp.float32)
                )
                part[k, ri, c, :, y] = total.astype(jnp.bfloat16)
        for step in (2, 1, 3):
            to = lax.rem(x + step, X)
            send(
                part.at[k, :, :, to % 2, y, to // 2], cross.at[k, step - 1], x_send, cross_recv.at[k], at_x(step)
            )

    def gather(k):
        await_bytes(cross.at[k], cross_recv.at[k])
        for ri in (0, 1):
            for c in range(per):
                at = k * per + c
                mine = part[k, ri, c, chan, y, x_hi].astype(jnp.float32) + cross[k, 1, ri, c].astype(jnp.float32)
                theirs = cross[k, 0, ri, c].astype(jnp.float32) + cross[k, 2, ri, c].astype(jnp.float32)
                half = channels // 2
                spread[pl.ds(ri * channels + chan * half + at, times, stride=2 * channels), :] = mine
                spread[pl.ds(ri * channels + (1 - chan) * half + at, times, stride=2 * channels), :] = theirs

    barrier = pltpu.get_barrier_semaphore()
    for other in others:
        pl.semaphore_signal(barrier, inc=1, device_id=other, device_id_type=MESH)

    @pl.loop(0, CHUNKS)
    def _(k):
        fetch_volt(k).start()

    @pl.loop(0, CHUNKS)
    def _(k):
        fetch_weight(k).start()

    pl.semaphore_wait(barrier, len(others))

    def stage(tick, lag, work):
        k = tick - lag

        @pl.when(jnp.logical_and(k >= 0, k < CHUNKS))
        def _():
            work(k)

    def first(k):
        fetch_volt(k).wait()
        z_hop(k, 0, 0)
        z_hop(k, 1, 0)

    def onward(distance):
        def work(k):
            z_hop(k, 0, distance)
            z_hop(k, 1, distance)

        return work

    def products(k):
        multiply(k)
        send_early(k)

    @pl.loop(0, CHUNKS + 9)
    def _(tick):
        stage(tick, 0, first)
        for distance in range(1, 5):
            stage(tick, distance, onward(distance))
        stage(tick, 5, products)
        stage(tick, 6, send_late)
        stage(tick, 7, send_cross)
        stage(tick, 8, gather)

    size = channels
    for t in range(0, times, 2):
        left = spread[t * 2 * size:(t + 1) * 2 * size, :].astype(jnp.bfloat16)
        right = spread[(t + 1) * 2 * size:(t + 2) * 2 * size, :].astype(jnp.bfloat16)
        fine = jnp.dot(table_ref[...], jnp.concatenate([left, right], axis=1), preferred_element_type=jnp.float32)
        real = fine[0:size] + fine[2 * size:3 * size]
        imag = fine[size:2 * size] + fine[3 * size:4 * size]
        power = real * real + imag * imag
        beams = power_ref.shape[1]
        power_ref[pl.ds(t, size, stride=times), :] = power[:, :beams]
        power_ref[pl.ds(t + 1, size, stride=times), :] = power[:, beams:]

    for side in (0, 1):
        await_bytes(volt.at[0, :, pl.ds(0, 7)], z_send.at[side])
        await_bytes(volt.at[0, :, pl.ds(0, 6)], y_send.at[side])
    await_bytes(volt.at[0], mate_send)
    await_bytes(volt.at[0, :, pl.ds(0, 3)], x_send)


def shards(voltages, weights):
    _, own, times, width = voltages.shape
    beams = weights.shape[3]
    owners = 2 * Z
    channels = 2 * own
    per = own // CHUNKS
    table = jnp.asarray(synthesis_table(channels))
    bf16, f32 = jnp.bfloat16, jnp.float32
    dma = pltpu.SemaphoreType.DMA
    power = pl.pallas_call(
        kernel,
        out_shape=jax.ShapeDtypeStruct((channels * times, beams), f32),
        in_specs=[
            pl.BlockSpec(memory_space=pl.ANY),
            pl.BlockSpec(memory_space=pl.ANY),
            pl.BlockSpec(memory_space=pltpu.VMEM),
        ],
        out_specs=pl.BlockSpec(memory_space=pltpu.VMEM),
        scratch_shapes=[
            pltpu.VMEM((2, own, owners, times, width), bf16),
            pltpu.VMEM((2, own, width, beams), bf16),
            pltpu.VMEM((CHUNKS, 2, per, 2, Y, 2, times, beams), bf16),
            pltpu.VMEM((CHUNKS, 2, per, 2, 2, times, beams), bf16),
            pltpu.VMEM((CHUNKS, 2, 2, per, 2, 2, times, beams), bf16),
            pltpu.VMEM((CHUNKS, 3, 2, per, times, beams), bf16),
            pltpu.VMEM((times * 2 * channels, beams), f32),
            dma((CHUNKS,)),
            dma((CHUNKS,)),
            dma((2, 4, CHUNKS)),
            dma((CHUNKS,)),
            dma((2, CHUNKS)),
            dma((2, CHUNKS)),
            dma((CHUNKS,)),
            dma((2,)),
            dma,
            dma((2,)),
            dma,
        ],
        compiler_params=pltpu.CompilerParams(
            collective_id=0, has_side_effects=True, vmem_limit_bytes=60 * 2**20
        ),
        name="beamform",
    )(voltages, weights, table)
    return power.reshape(channels, times, beams)


def solution(mesh):
    placed = (P(None, "chan", "beam", "elem"), P(None, "chan", "elem", "beam"))
    return jax.shard_map(
        shards,
        mesh=mesh,
        in_specs=placed,
        out_specs=P(None, ("chan", "elem"), "beam"),
        check_vma=False,
    )
```

time: 329 us -> 125 us (0.38)
  waiting for transfers between devices: 218 us -> 0 us
  Pallas kernels: 0 us -> 123 us
  matrix products: 46.4 us -> 0 us
  local copies, waits for them, and re-layouts: 23 us -> 2.26 us
  blocking collectives: 19.6 us -> 0 us
  between operations: 13.4 us -> 0.01 us
  other arithmetic: 7.45 us -> 0 us
    pallas_call x0 -> x1, Pallas kernels: none -> 123 us  [shards(): pl.pallas_call(kernel, out_shape=jax.ShapeDtypeStruct((channels * times,...]
    unnamed x3 -> x0, waiting for transfers between devices: 118 us -> none
    all_gather x1 -> x0, waiting for transfers between devices: 100 us -> none  [shards(): volt_piece = lax.all_gather(voltages, 'beam', axis=2, tiled=True)]
    dot_general x8 -> x0, matrix products: 46.4 us -> none  [the longest x1 11.4 us: shards(): jnp.einsum('cte,ceb->ctb', volt_piece[1], weights[0], preferred_element_t...]
    all_to_all x1 -> x0, blocking collectives: 19.6 us -> none  [shards(): lax.all_to_all(summed, ('chan', 'elem'), split_axis=2, concat_axis=1, til...]
    unnamed x4 -> x1, local copies, waits for them, and re-layouts: 21.3 us -> 2.26 us
    another operation x1 -> x0, other arithmetic: 7.45 us -> none  [shards(): partial_value = jnp.stack([real_part, imag_part])]
  transfers between devices with their start and end apart: 2 -> 0, of which waited for: 2 -> 0; matrix products, arithmetic and copies ran while one was open for 0% -> 0% of each run, Pallas kernels for 0% -> 0%
where the time goes in v1:
time: 125 us
  Pallas kernels  123 us (98%)
  local copies, waits for them, and re-layouts  2.26 us (2%)
    pallas_call x1, Pallas kernels, shards(): pl.pallas_call(kernel, out_shape=jax.ShapeDtypeStruct((channels * times,...  123 us

profile of v1, /device:TPU:8, one launch (start us, length us, event | category | flops | bytes accessed | tf_op | source)
XLA Modules:
  0.0 124.9 jit_solution(17553296310108244916)
XLA Ops:
  0.0 122.7 %beamform.1 = f32[2048,128]{1,0:T(8,128)} custom-call(bf16[2,64,16,256]{3,2,1,0:T(8,128)(2,1)} %volt_hbm.1, bf16[2,64,256,128]{3,2,1,0:T(8,128)(2,1)} %weight_hbm.1, bf16[512,256]{1,0:T(8,128)(2,1)} %constant.2.clone.table_ref), custom_call_target="tpu_custom_call" | custom-call | tf_op jit(solution)/shard_map/beamform/pallas_call | solution.py:240
  122.7 2.3 %copy.5 = f32[128,16,128]{2,1,0:T(8,128)} copy(f32[128,16,128]{2,1,0:T(8,128)} %bitcast.1) | data formatting | bytes 2097152

commit v2 on v0

v2 whole, which is shorter than its diff:
```python
import jax
import jax.numpy as jnp
import numpy as np
from jax import lax
from jax.experimental import pallas as pl
from jax.experimental.pallas import tpu as pltpu
from jax.sharding import PartitionSpec as P

MESH = pl.DeviceIdType.MESH

X, Y, Z = 4, 4, 8
CHUNKS = ((20, 3), (2, 2))
ORDER = (('products', 7), (3, 5), (4, 6), ('mate', 6), (0, 0), ('late', 8), (1, 2), ('gather', 14), ('cross', 10), (2, 3))


def synthesis_table(channels):
    index = np.arange(channels)
    angle = (index[:, None] * index[None, :] % channels) * (2.0 * np.pi / channels)
    cosine, sine = np.cos(angle) / np.sqrt(channels), np.sin(angle) / np.sqrt(channels)
    table = np.block([[cosine, -sine], [sine, cosine]]).astype(np.float32)
    high = table.astype(jnp.bfloat16)
    low = (table - high.astype(np.float32)).astype(jnp.bfloat16)
    return np.concatenate([high, low], axis=0)


def kernel(
    volt_hbm, weight_hbm, table_hbm, power_ref,
    volt, weight, part, early, late, cross, spread, table,
    volt_in, weight_in, table_in, z_recv, mate_recv, early_recv, late_recv, cross_recv,
    z_send, mate_send, y_send, x_send,
):
    chan, elem, beam = lax.axis_index("chan"), lax.axis_index("elem"), lax.axis_index("beam")
    z, core = beam // 2, beam % 2
    y, x_hi = elem // 2, elem % 2
    x = x_hi * 2 + chan
    times = volt.shape[4]
    channels = 2 * volt.shape[0]
    chunks = sum(count for count, _ in CHUNKS)

    def at_z(step):
        return (chan, elem, lax.rem(z + step + Z, Z) * 2 + core)

    def at_y(step):
        return (chan, lax.rem(y + step + Y, Y) * 2 + x_hi, beam)

    def at_x(step):
        to = lax.rem(x + step, X)
        return (to % 2, y * 2 + to // 2, beam)

    mate = (chan, elem, z * 2 + (1 - core))
    others = [mate, at_z(1), at_z(-1), at_y(1), at_y(-1), at_x(1), at_x(2), at_x(3)]

    def fetch_volt(k, at):
        for ri in (0, 1):
            pltpu.make_async_copy(volt_hbm.at[ri, at], volt.at[at, core, z, ri], volt_in.at[k]).start()

    def fetch_weight(k, at):
        return pltpu.make_async_copy(weight_hbm.at[:, at], weight.at[:, at], weight_in.at[k])

    fetch_table = pltpu.make_async_copy(table_hbm, table, table_in)

    def send(src, dst, send_sem, recv_sem, to):
        pltpu.make_async_remote_copy(
            src_ref=src, dst_ref=dst, send_sem=send_sem, recv_sem=recv_sem, device_id=to, device_id_type=MESH
        ).start()

    def await_bytes(like, sem):
        pltpu.make_async_copy(like, like, sem).wait()

    def piece(at, owner, half=None):
        return volt.at[at, core, owner] if half is None else volt.at[at, core, owner, half]

    def z_hop(k, at, side, distance):
        owner = lax.rem(z + (distance if side else -distance) + Z, Z)
        if distance:
            await_bytes(piece(at, owner, side if distance == 4 else None), z_recv.at[side, distance - 1, k])
        if distance < 4:
            moved = piece(at, owner, side if distance == 3 else None)
            send(moved, moved, z_send.at[side], z_recv.at[side, distance, k], at_z(-1 if side else 1))

    def to_y(step):
        return lax.rem(y + step + Y, Y)

    def multiply(k, at):
        fetch_weight(k, at).wait()
        await_bytes(volt.at[at, 0], mate_recv.at[k])

        @pl.loop(0, at.size)
        def _(step):
            c = at.start + step
            width, beams = volt.shape[5], weight.shape[3]
            both = jnp.concatenate([weight[0, c], weight[1, c]], axis=1)

            def times_both(ri):
                rows = jnp.stack([volt[c, 0, :, ri], volt[c, 1, :, ri]], axis=1)
                return jnp.dot(rows.reshape(2 * Z * times, width), both, preferred_element_type=jnp.float32)

            with_real, with_imag = times_both(0), times_both(1)
            real = (with_real[:, :beams] - with_imag[:, beams:]).astype(jnp.bfloat16)
            imag = (with_real[:, beams:] + with_imag[:, :beams]).astype(jnp.bfloat16)
            for ri, value in enumerate((real, imag)):
                value = value.reshape(2, Y, 2, times, beams)
                for lo in (0, 1):
                    part[c, :, ri, lo] = value[lo]

    def send_mate(k, at):
        send(volt.at[at, core], volt.at[at, core], mate_send, mate_recv.at[k], mate)

    def send_early(k, at):
        for side in (0, 1):
            send(
                part.at[at, to_y(2), side], early.at[at, side], y_send.at[side], early_recv.at[side, k],
                at_y(-1 if side else 1),
            )

    def send_late(k, at):
        for side in (0, 1):
            near = to_y(-1 if side else 1)
            await_bytes(early.at[at, side], early_recv.at[side, k])
            total = part[at, near, side].astype(jnp.float32) + early[at, side].astype(jnp.float32)
            part[at, near, side] = total.astype(jnp.bfloat16)
            send(
                part.at[at, near], late.at[at, side], y_send.at[side], late_recv.at[side, k], at_y(-1 if side else 1)
            )

    def send_cross(k, at):
        for side in (0, 1):
            await_bytes(late.at[at, side], late_recv.at[side, k])
        total = part[at, y].astype(jnp.float32) + late[at, 0].astype(jnp.float32) + late[at, 1].astype(jnp.float32)
        part[at, y] = total.astype(jnp.bfloat16)
        for step in (2, 1, 3):
            to = lax.rem(x + step, X)
            send(
                part.at[at, y, :, to % 2, to // 2], cross.at[at, step - 1], x_send, cross_recv.at[k], at_x(step)
            )

    def gather(k, at):
        await_bytes(cross.at[at], cross_recv.at[k])
        half = channels // 2
        for ri in (0, 1):
            for step in range(at.size):
                c = at.start + step
                row = ri * channels + c
                mine = part[c, y, ri, chan, x_hi].astype(jnp.float32) + cross[c, 1, ri].astype(jnp.float32)
                theirs = cross[c, 0, ri].astype(jnp.float32) + cross[c, 2, ri].astype(jnp.float32)
                spread[pl.ds(chan * half + row, times, stride=2 * channels), :] = mine
                spread[pl.ds((1 - chan) * half + row, times, stride=2 * channels), :] = theirs

    def in_chunk(k, work):
        chunk, channel = 0, 0
        for count, size in CHUNKS:

            @pl.when(jnp.logical_and(k >= chunk, k < chunk + count))
            def _():
                work(k, pl.ds(channel + (k - chunk) * size, size))

            chunk, channel = chunk + count, channel + count * size

    barrier = pltpu.get_barrier_semaphore()
    for other in others:
        pl.semaphore_signal(barrier, inc=1, device_id=other, device_id_type=MESH)

    @pl.loop(0, chunks)
    def _(k):
        in_chunk(k, fetch_volt)

    @pl.loop(0, chunks)
    def _(k):
        in_chunk(k, lambda k, at: fetch_weight(k, at).start())

    fetch_table.start()
    pl.semaphore_wait(barrier, len(others))

    def z_stage(distance):
        def work(k, at):
            if distance == 0:
                await_bytes(piece(at, z), volt_in.at[k])
            for side in (0, 1):
                z_hop(k, at, side, distance)

        return work

    def products(k, at):
        multiply(k, at)
        send_early(k, at)

    stages = {"mate": send_mate, "products": products, "late": send_late, "cross": send_cross, "gather": gather}
    stages.update((distance, z_stage(distance)) for distance in range(5))

    @pl.loop(0, chunks + max(lag for _, lag in ORDER))
    def _(tick):
        for stage, lag in ORDER:
            in_chunk(tick - lag, stages[stage])

    fetch_table.wait()

    size = channels
    for t in range(0, times, 2):
        left = spread[t * 2 * size:(t + 1) * 2 * size, :].astype(jnp.bfloat16)
        right = spread[(t + 1) * 2 * size:(t + 2) * 2 * size, :].astype(jnp.bfloat16)
        fine = jnp.dot(table[...], jnp.concatenate([left, right], axis=1), preferred_element_type=jnp.float32)
        real = fine[0:size] + fine[2 * size:3 * size]
        imag = fine[size:2 * size] + fine[3 * size:4 * size]
        power = real * real + imag * imag
        beams = power_ref.shape[1]
        power_ref[pl.ds(t, size, stride=times), :] = power[:, :beams]
        power_ref[pl.ds(t + 1, size, stride=times), :] = power[:, beams:]

    for side in (0, 1):
        await_bytes(volt.at[:, 0, 0:7, 0], z_send.at[side])
        await_bytes(volt.at[:, 0, 0:3], y_send.at[side])
    await_bytes(volt.at[:, 0], mate_send)
    await_bytes(cross, x_send)


def shards(voltages, weights):
    _, own, times, width = voltages.shape
    beams = weights.shape[3]
    channels = 2 * own
    chunks = sum(count for count, _ in CHUNKS)
    table = jnp.asarray(synthesis_table(channels))
    bf16, f32 = jnp.bfloat16, jnp.float32
    dma = pltpu.SemaphoreType.DMA
    power = pl.pallas_call(
        kernel,
        out_shape=jax.ShapeDtypeStruct((channels * times, beams), f32),
        in_specs=[pl.BlockSpec(memory_space=pltpu.HBM)] * 3,
        out_specs=pl.BlockSpec(memory_space=pltpu.VMEM),
        scratch_shapes=[
            pltpu.VMEM((own, 2, Z, 2, times, width), bf16),
            pltpu.VMEM((2, own, width, beams), bf16),
            pltpu.VMEM((own, Y, 2, 2, 2, times, beams), bf16),
            pltpu.VMEM((own, 2, 2, 2, times, beams), bf16),
            pltpu.VMEM((own, 2, 2, 2, 2, times, beams), bf16),
            pltpu.VMEM((own, 3, 2, times, beams), bf16),
            pltpu.VMEM((times * 2 * channels, beams), f32),
            pltpu.VMEM(table.shape, bf16),
            dma((chunks,)),
            dma((chunks,)),
            dma,
            dma((2, 4, chunks)),
            dma((chunks,)),
            dma((2, chunks)),
            dma((2, chunks)),
            dma((chunks,)),
            dma((2,)),
            dma,
            dma((2,)),
            dma,
        ],
        compiler_params=pltpu.CompilerParams(
            collective_id=0, has_side_effects=True, vmem_limit_bytes=46 * 2**20
        ),
        name="beamform",
    )(voltages, weights, table)
    return power.reshape(channels, times, beams)


def solution(mesh):
    placed = (P(None, "chan", "beam", "elem"), P(None, "chan", "elem", "beam"))
    return jax.shard_map(
        shards,
        mesh=mesh,
        in_specs=placed,
        out_specs=P(None, ("chan", "elem"), "beam"),
        check_vma=False,
    )
```

time: 329 us -> 116 us (0.35)
  waiting for transfers between devices: 218 us -> 0 us
  Pallas kernels: 0 us -> 113 us
  matrix products: 46.4 us -> 0 us
  local copies, waits for them, and re-layouts: 23 us -> 3.15 us
  blocking collectives: 19.6 us -> 0 us
  between operations: 13.4 us -> 0.01 us
  other arithmetic: 7.45 us -> 0 us
    unnamed x3 -> x0, waiting for transfers between devices: 118 us -> none
    pallas_call x0 -> x1, Pallas kernels: none -> 113 us  [shards(): pl.pallas_call(kernel, out_shape=jax.ShapeDtypeStruct((channels * times,...]
    all_gather x1 -> x0, waiting for transfers between devices: 100 us -> none  [shards(): volt_piece = lax.all_gather(voltages, 'beam', axis=2, tiled=True)]
    dot_general x8 -> x0, matrix products: 46.4 us -> none  [the longest x1 11.4 us: shards(): jnp.einsum('cte,ceb->ctb', volt_piece[1], weights[0], preferred_element_t...]
    all_to_all x1 -> x0, blocking collectives: 19.6 us -> none  [shards(): lax.all_to_all(summed, ('chan', 'elem'), split_axis=2, concat_axis=1, til...]
    unnamed x4 -> x5, local copies, waits for them, and re-layouts: 21.3 us -> 3.15 us
    another operation x1 -> x0, other arithmetic: 7.45 us -> none  [shards(): partial_value = jnp.stack([real_part, imag_part])]
  transfers between devices with their start and end apart: 2 -> 0, of which waited for: 2 -> 0; matrix products, arithmetic and copies ran while one was open for 0% -> 0% of each run, Pallas kernels for 0% -> 0%
where the time goes in v2:
time: 116 us
  Pallas kernels  113 us (97%)
  local copies, waits for them, and re-layouts  3.15 us (3%)
    pallas_call x1, Pallas kernels, shards(): pl.pallas_call(kernel, out_shape=jax.ShapeDtypeStruct((channels * times,...  113 us
    unnamed x5, local copies, waits for them, and re-layouts  3.15 us

profile of v2, /device:TPU:8, one launch (start us, length us, event | category | flops | bytes accessed | tf_op | source)
XLA Modules:
  0.0 115.9 jit_solution(6975530186831027797)
XLA Ops:
  0.0 0.0 copy-start
  0.0 1.2 %copy-done = bf16[2,64,16,256]{3,2,1,0:T(8,128)(2,1)S(1)} copy-done((bf16[2,64,16,256]{3,2,1,0:T(8,128)(2,1)S(1)}, bf16[2,64,16,256]{3,2,1,0:T(8,128)(2,1)}, u32[]{:S(2)}) %copy-start) | copy-done | bytes 1048600
  1.2 0.0 copy-start.1
  1.2 0.9 copy-done.1
  2.2 112.7 %beamform.1 = f32[2048,128]{1,0:T(8,128)S(1)} custom-call(bf16[2,64,16,256]{3,2,1,0:T(8,128)(2,1)S(1)} %copy-done, bf16[2,64,256,128]{3,2,1,0:T(8,128)(2,1)} %weight_hbm.1, bf16[512,256]{1,0:T(8,128)(2,1)S(1)} %copy-done.1), custom_call_target="tpu_custom_call" | custom-call | tf_op jit(solution)/shard_map/beamform/pallas_call | solution.py:224
  114.9 1.0 copy.5
Async XLA Ops:
  0.0 1.2 %copy-start = (bf16[2,64,16,256]{3,2,1,0:T(8,128)(2,1)S(1)}, bf16[2,64,16,256]{3,2,1,0:T(8,128)(2,1)}, u32[]{:S(2)}) copy-start(bf16[2,64,16,256]{3,2,1,0:T(8,128)(2,1)} %volt_hbm.1) | copy-start | bytes 3145732
  1.2 0.9 copy-start.1

commit v3 on v2

--- a/solution.py
+++ b/solution.py
@@ -9,8 +9,8 @@
 MESH = pl.DeviceIdType.MESH
 
 X, Y, Z = 4, 4, 8
-CHUNKS = ((20, 3), (2, 2))
-ORDER = (('products', 7), (3, 5), (4, 6), ('mate', 6), (0, 0), ('late', 8), (1, 2), ('gather', 14), ('cross', 10), (2, 3))
+CHUNKS = ((18, 3), (5, 2))
+ORDER = ((3, 5), (4, 6), ('mate', 6), ('gather', 14), ('late', 8), (0, 0), (1, 2), ('cross', 10), (2, 3), ('products', 6))
 
 
 def synthesis_table(channels):
@@ -252,7 +252,7 @@
             collective_id=0, has_side_effects=True, vmem_limit_bytes=46 * 2**20
         ),
         name="beamform",
-    )(voltages, weights, table)
+    )(*(pltpu.with_memory_space_constraint(v, pltpu.HBM) for v in (voltages, weights, table)))
     return power.reshape(channels, times, beams)
 
 

time: 116 us -> 114 us (0.983)
  local copies, waits for them, and re-layouts: 3.15 us -> 0.97 us
    unnamed x5 -> x1, local copies, waits for them, and re-layouts: 3.15 us -> 0.97 us
where the time goes in v3:
time: 114 us
  Pallas kernels  113 us (99%)
    pallas_call x1, Pallas kernels, shards(): pl.pallas_call(kernel, out_shape=jax.ShapeDtypeStruct((channels * times,...  113 us

profile of v3, /device:TPU:8, one launch (start us, length us, event | category | flops | bytes accessed | tf_op | source)
XLA Modules:
  0.0 113.9 jit_solution(11453896253668617592)
XLA Ops:
  0.0 112.9 %beamform.1 = f32[2048,128]{1,0:T(8,128)S(1)} custom-call(bf16[2,64,16,256]{3,2,1,0:T(8,128)(2,1)} %volt_hbm.1, bf16[2,64,256,128]{3,2,1,0:T(8,128)(2,1)} %weight_hbm.1, bf16[512,256]{1,0:T(8,128)(2,1)} %constant.2.clone.table_hbm), custom_call_target="tpu_custom_call" | custom-call | tf_op jit(solution)/shard_map/beamform/pallas_call | solution.py:224
  112.9 1.0 copy.5

commit v4 on v3

--- a/solution.py
+++ b/solution.py
@@ -112,6 +112,13 @@
                 part.at[at, to_y(2), side], early.at[at, side], y_send.at[side], early_recv.at[side, k],
                 at_y(-1 if side else 1),
             )
+        if at.size < CHUNKS[0][1]:
+            for side in (0, 1):
+                near, half = to_y(-1 if side else 1), 1 - side
+                send(
+                    part.at[at, near, half], late.at[at, side, half], y_send.at[side], late_recv.at[side, k],
+                    at_y(-1 if side else 1),
+                )
 
     def send_late(k, at):
         for side in (0, 1):
@@ -119,8 +126,11 @@
             await_bytes(early.at[at, side], early_recv.at[side, k])
             total = part[at, near, side].astype(jnp.float32) + early[at, side].astype(jnp.float32)
             part[at, near, side] = total.astype(jnp.bfloat16)
+            whole = at.size == CHUNKS[0][1]
             send(
-                part.at[at, near], late.at[at, side], y_send.at[side], late_recv.at[side, k], at_y(-1 if side else 1)
+                part.at[at, near] if whole else part.at[at, near, side],
+                late.at[at, side] if whole else late.at[at, side, side],
+                y_send.at[side], late_recv.at[side, k], at_y(-1 if side else 1),
             )
 
     def send_cross(k, at):

time: 114 us -> 114 us (level)
  no operation moved by 1% of the time
where the time goes in v4:
time: 114 us
  Pallas kernels  113 us (99%)
    pallas_call x1, Pallas kernels, shards(): pl.pallas_call(kernel, out_shape=jax.ShapeDtypeStruct((channels * times,...  113 us

profile of v4, /device:TPU:8, one launch (start us, length us, event | category | flops | bytes accessed | tf_op | source)
XLA Modules:
  0.0 113.8 jit_solution(17431040726935607501)
XLA Ops:
  0.0 112.8 %beamform.1 = f32[2048,128]{1,0:T(8,128)S(1)} custom-call(bf16[2,64,16,256]{3,2,1,0:T(8,128)(2,1)} %volt_hbm.1, bf16[2,64,256,128]{3,2,1,0:T(8,128)(2,1)} %weight_hbm.1, bf16[512,256]{1,0:T(8,128)(2,1)} %constant.2.clone.table_hbm), custom_call_target="tpu_custom_call" | custom-call | tf_op jit(solution)/shard_map/beamform/pallas_call | solution.py:234
  112.8 1.0 copy.5
